TPU v7x, 128 devices: a whole 4x4x4 slice. The times are simulated.
128 devices in a mesh: gy: 16 (over z, y_lo, core), gx: 8 (over x, y_hi).
Axes of the slice: x: 4, y: 4 (y_hi: 2, y_lo: 2; y = y_hi * 2 + y_lo), z: 4, core: 2. Of those that a mesh axis runs over, the one named last changes fastest.
Arguments:
- mean_util: float32 [32, 128, 256], P(None, 'gy', 'gx'), may hold values from -4 to 4
- observed_shares: float32 [32, 128, 256], P(None, 'gy', 'gx'), may hold values from 0.002 to 0.02
- characteristics: float32 [4, 32, 128, 256], P(None, None, 'gy', 'gx'), may hold values from -2 to 2
- taste_draws: float32 [4, 512], replicated, may hold values from -4 to 4
- taste_scale: float32 [4], replicated, may hold values from 0.3 to 1
- prior_probs: bfloat16 [32, 128, 256, 512], P(None, 'gy', 'gx'), may hold values from 0 to 0.099609375
- spill_rate: float32 [32], replicated, may hold values from 1 to 8
- utility_rate: float32 [32], replicated, may hold values from 0.1 to 0.6
- adjacency: int32 [4, 128, 256], P(None, 'gy', 'gx'), may hold values from 0 to 3
Outputs:
- final_util: float32 [32, 128, 256], P(None, 'gy', 'gx')
- log_shares: float32 [32, 128, 256], P(None, 'gy', 'gx')
- residual_max: float32 [3], replicated
All inputs are finite; a program needn't handle non-finite values. Where the computation divides by a largest or mean magnitude, that divisor is 1e-20 or more.
Results may differ from a plain program's by a relative error of at most 0.0008.
Values may be sent and summed in bfloat16 or wider, within the bound.
A program may use at most 192 MiB of HBM per device.

v0:
```python
import functools
import math

import jax
import jax.numpy as jnp
from jax import lax
from jax.experimental import pallas as pl
from jax.experimental.pallas import tpu as pltpu
from jax.sharding import PartitionSpec as P

ITERS = 3
J = 32
K = 4
TR = 8
TC = 32
M = TR * TC
HM = M // 2
R = 512
RC = 128
NC = R // RC
NY = 16
NX = 8
LOG2E = math.log2(math.e)
step_level = 0.2
gap_eps = 1e-06
MESH = pl.DeviceIdType.MESH
F32 = jnp.float32
BF16 = jnp.bfloat16


def lane_iota(shape):
    return lax.broadcasted_iota(jnp.int32, shape, len(shape) - 1)


def row_iota(shape):
    return lax.broadcasted_iota(jnp.int32, shape, len(shape) - 2)


def exact_dot(a, b, dims):
    return lax.dot_general(
        a, b, (dims, ((), ())), precision=lax.Precision.HIGHEST, preferred_element_type=F32
    )


def kernel(
    mean_in, obs_in, chars_in, draws_ref, scale_ref, prior_in, spill_ref, rate_ref, adj_ref,
    mean_out, log_out, gap_out,
    st, hr, hc, cs, taste, ex, bx, den, rden, amat, aw, inv, gain, cz, char_buf,
    zmean, zobs, zlog, zsend, zc_send, hz_r, hz_c, mh_r, mh_c, share, mxs, mxg, mxy,
    prior_sem, char_sem, s_sem, r_sem, sz_sem, rz_sem, sg_sem, rg_sem, sy_sem, ry_sem,
):
    gy = lax.axis_index("gy")
    gx = lax.axis_index("gx")

    def prior_copy(c):
        return pltpu.make_async_copy(
            prior_in.at[:, :, :, pl.ds(pl.multiple_of(c * RC, RC), RC)], st.at[0, c], prior_sem.at[c]
        )

    for c in range(NC):
        prior_copy(c).start()
    char_copy = pltpu.make_async_copy(chars_in, char_buf, char_sem)
    char_copy.start()

    barrier = pltpu.get_barrier_semaphore()
    for d in range(1, NX):
        pl.semaphore_signal(
            barrier, inc=1, device_id={"gx": lax.rem(gx + d, NX)}, device_id_type=MESH
        )
    for d in range(1, NY):
        pl.semaphore_signal(
            barrier, inc=1, device_id={"gy": lax.rem(gy + d, NY)}, device_id_type=MESH
        )
    pl.semaphore_wait(barrier, NX - 1 + NY - 1)

    north = {"gy": lax.rem(gy + NY - 1, NY)}
    south = {"gy": lax.rem(gy + 1, NY)}
    west = {"gx": lax.rem(gx + NX - 1, NX)}
    east = {"gx": lax.rem(gx + 1, NX)}

    def edge_copies(e, c):
        b = e % 2
        plan = (
            (st.at[b, c, :, TR - 1], hr.at[e, c, 0], south),
            (st.at[b, c, :, 0], hr.at[e, c, 1], north),
            (cs.at[e, c, 1], hc.at[e, c, 0], east),
            (cs.at[e, c, 0], hc.at[e, c, 1], west),
        )
        return [
            pltpu.make_async_remote_copy(
                src_ref=src, dst_ref=dst, send_sem=s_sem.at[e, c, k], recv_sem=r_sem.at[e, c, k],
                device_id=to, device_id_type=MESH,
            )
            for k, (src, dst, to) in enumerate(plan)
        ]

    def small_copies(x):
        plan = (
            (zsend.at[x, pl.ds(M - TC, TC)], hz_r.at[x, 0], south),
            (zsend.at[x, pl.ds(0, TC)], hz_r.at[x, 1], north),
            (zc_send.at[x, 1], hz_c.at[x, 0], east),
            (zc_send.at[x, 0], hz_c.at[x, 1], west),
        )
        return [
            pltpu.make_async_remote_copy(
                src_ref=src, dst_ref=dst, send_sem=sz_sem.at[x, k], recv_sem=rz_sem.at[x, k],
                device_id=to, device_id_type=MESH,
            )
            for k, (src, dst, to) in enumerate(plan)
        ]

    def send_small(x, value):
        zsend[x] = value
        zc_send[x, 0] = zsend[x, pl.ds(0, TR, stride=TC), :]
        zc_send[x, 1] = zsend[x, pl.ds(TC - 1, TR, stride=TC), :]
        for copy in small_copies(x):
            copy.start()

    @pl.loop(0, NC)
    def _(c):
        prior_copy(c).wait()

        @pl.loop(0, J // 2)
        def _(q):
            west_cols = []
            east_cols = []
            for jj in range(2):
                j = 2 * q + jj
                value = st[0, c, j].reshape(M, RC).astype(F32) * spill_ref[j]
                st[0, c, j] = value.astype(BF16).reshape(TR, TC, RC)
                ex[j] = value
                west_cols.append(ex[j, pl.ds(0, TR, stride=TC), :])
                east_cols.append(ex[j, pl.ds(TC - 1, TR, stride=TC), :])
            cs[0, c, 0, q] = jnp.concatenate(west_cols, axis=0).astype(BF16)
            cs[0, c, 1, q] = jnp.concatenate(east_cols, axis=0).astype(BF16)

        for copy in edge_copies(0, c):
            copy.start()

    eye = (row_iota((TC, TC)) == lane_iota((TC, TC))).astype(F32)
    eye_wide = (row_iota((J, 128)) == lane_iota((J, 128))).astype(F32)
    pad = jnp.zeros((128 - J, TC), F32)

    def to_markets(block):
        return exact_dot(eye, jnp.concatenate([block, pad], axis=0), ((1,), (1,)))

    for row in range(TR):
        rows = pl.ds(row * TC, TC)
        zmean[rows, :] = to_markets(mean_in[:, row, :])
        zobs[rows, :] = to_markets(jnp.log(obs_in[:, row, :]))
    send_small(0, zmean[...])

    for k in range(4):
        for row in range(TR):
            line = adj_ref[k, pl.ds(row, 1), :].astype(F32)
            column = jnp.sum(jnp.where(eye > 0, line, 0.0), axis=1, keepdims=True)
            aw[k, pl.ds(row * TC, TC), :] = jnp.broadcast_to(column, (TC, 128))
    links = jnp.maximum(aw[0] + aw[1] + aw[2] + aw[3], 1.0)
    inverse = 1.0 / links
    inv[...] = inverse
    gain[...] = inverse * LOG2E

    @pl.loop(0, 4)
    def _(i):
        par = i // 2
        h = i % 2
        shape = (HM, 128)
        at = row_iota(shape)
        col = at & (TC - 1)
        row = (at >> 5) + h * (TR // 2)
        mrows = pl.ds(pl.multiple_of(h * HM, HM), HM)
        w0 = jnp.where((row == 0) & (gy == 0), 0.0, aw[0, mrows, :])
        w1 = jnp.where((row == TR - 1) & (gy == NY - 1), 0.0, aw[1, mrows, :])
        w2 = jnp.where((col == 0) & (gx == 0), 0.0, aw[2, mrows, :])
        w3 = jnp.where((col == TC - 1) & (gx == NX - 1), 0.0, aw[3, mrows, :])
        west_slot = jnp.where(col == 0, 192 + par * TR + row, at + TC - 1)
        east_slot = jnp.where(col == TC - 1, 208 + par * TR + row, at + TC + 1)
        for part in range(2):
            slot = lane_iota(shape) + part * 128
            entry = jnp.where(slot == at, w0, 0.0)
            entry = entry + jnp.where(slot == at + 2 * TC, w1, 0.0)
            entry = entry + jnp.where(slot == west_slot, w2, 0.0)
            entry = entry + jnp.where(slot == east_slot, w3, 0.0)
            amat[par, h, :, pl.ds(part * 128, 128)] = entry.astype(BF16)

    char_copy.wait()

    @pl.loop(0, K)
    def _(k):
        for row in range(TR):
            cz[k, pl.ds(row * TC, TC), :] = to_markets(char_buf[k, :, row, :])

    draw_rows = [
        [draws_ref[pl.ds(k, 1), pl.ds(c * RC, RC)] * (scale_ref[k] * LOG2E) for c in range(NC)]
        for k in range(K)
    ]

    @pl.loop(0, J)
    def _(j):
        @pl.loop(0, TR)
        def _(row):
            rows = pl.ds(pl.multiple_of(row * TC, TC), TC)
            here = lane_iota((TC, 128)) == j
            columns = [
                jnp.sum(jnp.where(here, cz[k, rows, :], 0.0), axis=1, keepdims=True) for k in range(K)
            ]
            for c in range(NC):
                total = columns[0] * draw_rows[0][c]
                for k in range(1, K):
                    total = total + columns[k] * draw_rows[k][c]
                taste[c, j, rows, :] = total

    rates = jnp.zeros((1, 128), F32)
    for j in range(J):
        rates = jnp.where(lane_iota((1, 128)) == j, rate_ref[j], rates)
    real = lane_iota((M, 128)) < J
    zero_rows = jnp.zeros((TR, 128), F32)
    zero_tail = jnp.zeros((32, 128), F32)

    def largest(t, value):
        mxs[t, 0] = value
        mxg[t, gx] = value

        def along_x(d):
            return pltpu.make_async_remote_copy(
                src_ref=mxs.at[t, 0], dst_ref=mxg.at[t, gx], send_sem=sg_sem.at[t, d],
                recv_sem=rg_sem.at[t, gx], device_id={"gx": lax.rem(gx + d, NX)}, device_id_type=MESH,
            )

        def from_x(d):
            k = lax.rem(gx + d, NX)
            return pltpu.make_async_remote_copy(
                src_ref=mxs.at[t, 0], dst_ref=mxg.at[t, k], send_sem=sg_sem.at[t, d],
                recv_sem=rg_sem.at[t, k], device_id={"gx": k}, device_id_type=MESH,
            )

        def along_y(d):
            return pltpu.make_async_remote_copy(
                src_ref=mxs.at[t, 1], dst_ref=mxy.at[t, gy], send_sem=sy_sem.at[t, d],
                recv_sem=ry_sem.at[t, gy], device_id={"gy": lax.rem(gy + d, NY)}, device_id_type=MESH,
            )

        def from_y(d):
            k = lax.rem(gy + d, NY)
            return pltpu.make_async_remote_copy(
                src_ref=mxs.at[t, 1], dst_ref=mxy.at[t, k], send_sem=sy_sem.at[t, d],
                recv_sem=ry_sem.at[t, k], device_id={"gy": k}, device_id_type=MESH,
            )

        for d in range(1, NX):
            along_x(d).start()
        for d in range(1, NX):
            from_x(d).wait_recv()
        best = mxg[t, 0]
        for k in range(1, NX):
            best = jnp.maximum(best, mxg[t, k])
        mxs[t, 1] = best
        mxy[t, gy] = best
        for d in range(1, NY):
            along_y(d).start()
        for d in range(1, NY):
            from_y(d).wait_recv()
        best = mxy[t, 0]
        for k in range(1, NY):
            best = jnp.maximum(best, mxy[t, k])
        for d in range(1, NX):
            along_x(d).wait_send()
        for d in range(1, NY):
            along_y(d).wait_send()
        return best

    for copy in small_copies(0):
        copy.wait()
    mh_r[...] = hz_r[0]
    mh_c[...] = hz_c[0]

    for t in range(ITERS):
        b = t % 2
        last = t == ITERS - 1

        mean_now = zmean[...]
        west_halo = [mh_c[0], zero_rows]
        east_halo = [mh_c[1], zero_rows]
        for h in range(2):
            if h == 0:
                pieces = [mh_r[0], mean_now[: 5 * TC]]
            else:
                pieces = [mean_now[3 * TC :], mh_r[1]]
            around = jnp.concatenate(pieces + west_halo + east_halo + [zero_tail], axis=0)
            part = exact_dot(amat[0, h].astype(F32), around, ((1,), (0,)))
            rows = pl.ds(h * HM, HM)
            zlog[rows, :] = (zmean[rows, :] + rates * (part * inv[rows, :])) * LOG2E

        @pl.loop(0, J)
        def _(j):
            picked = jnp.where(lane_iota((M, 128)) == j, zlog[...], 0.0)
            bx[j] = jnp.broadcast_to(jnp.sum(picked, axis=1, keepdims=True), (M, 128))

        share[...] = jnp.zeros((M, 128), F32)

        @pl.loop(0, NC)
        def _(c):
            for copy in edge_copies(t, c):
                copy.wait_recv()
            den[...] = jnp.ones((M, RC), F32)

            @pl.loop(0, J // 2)
            def _(q):
                halo_cols = [hc[t, c, 0, q], hc[t, c, 1, q], jnp.zeros((32, RC), BF16)]
                for h in range(2):
                    rows = pl.ds(h * HM, HM)
                    total = den[rows, :]
                    for jj in range(2):
                        j = 2 * q + jj
                        if h == 0:
                            pieces = [hr[t, c, 0, j], st[b, c, j, pl.ds(0, 5)].reshape(5 * TC, RC)]
                        else:
                            pieces = [st[b, c, j, pl.ds(3, 5)].reshape(5 * TC, RC), hr[t, c, 1, j]]
                        around = jnp.concatenate(pieces + halo_cols, axis=0)
                        spill = lax.dot_general(
                            amat[jj, h], around, (((1,), (0,)), ((), ())), preferred_element_type=F32
                        )
                        power = spill * gain[rows, :] + (taste[c, j, rows, :] + bx[j, rows, :])
                        value = jnp.exp2(power)
                        ex[j, rows, :] = value
                        total = total + value
                    den[rows, :] = total

            rden[...] = 1.0 / den[...]
            if t == 1:
                for copy in edge_copies(0, c):
                    copy.wait_send()

            @pl.loop(0, J // 2)
            def _(q):
                west_cols = []
                east_cols = []
                for jj in range(2):
                    j = 2 * q + jj
                    for h in range(2):
                        rows = pl.ds(h * HM, HM)
                        prob = ex[j, rows, :] * rden[rows, :]
                        here = lane_iota((HM, 128)) == j
                        share[rows, :] += jnp.where(here, jnp.sum(prob, axis=1, keepdims=True), 0.0)
                        if not last:
                            st[1 - b, c, j, pl.ds(h * (TR // 2), TR // 2)] = (
                                (prob * spill_ref[j]).astype(BF16).reshape(TR // 2, TC, RC)
                            )
                    if not last:
                        for cols, first in ((west_cols, 0), (east_cols, TC - 1)):
                            at = pl.ds(first, TR, stride=TC)
                            cols.append(ex[j, at, :] * rden[at, :] * spill_ref[j])
                if not last:
                    cs[t + 1, c, 0, q] = jnp.concatenate(west_cols, axis=0).astype(BF16)
                    cs[t + 1, c, 1, q] = jnp.concatenate(east_cols, axis=0).astype(BF16)

            if not last:
                for copy in edge_copies(t + 1, c):
                    copy.start()

        log_share = jnp.log(jnp.where(real, share[...] * (1.0 / R), 1.0))
        residual = jnp.where(real, zobs[...] - log_share, 0.0)
        if not last:
            send_small(t + 1, residual)
        gap = jnp.max(jnp.max(jnp.abs(residual), axis=0, keepdims=True), axis=1, keepdims=True)
        if last:
            for row in range(TR):
                log_out[:, row, :] = exact_dot(
                    eye_wide, log_share[row * TC : (row + 1) * TC], ((1,), (1,))
                )
        best = largest(t, jnp.broadcast_to(gap, (1, 128)))
        gap_out[t] = jnp.max(best)
        step = step_level / (best + gap_eps)
        mean_now = zmean[...] + step * residual
        if not last:
            zmean[...] = mean_now
            for copy in small_copies(t + 1):
                copy.wait()
            mh_r[...] = mh_r[...] + step * hz_r[t + 1]
            mh_c[...] = mh_c[...] + step * hz_c[t + 1]
        else:
            for row in range(TR):
                mean_out[:, row, :] = exact_dot(
                    eye_wide, mean_now[row * TC : (row + 1) * TC], ((1,), (1,))
                )

    for e in range(1, ITERS):
        @pl.loop(0, NC)
        def _(c):
            for copy in edge_copies(e, c):
                copy.wait_send()


def local(*args):
    vmem = pl.BlockSpec(memory_space=pltpu.VMEM)
    smem = pl.BlockSpec(memory_space=pltpu.SMEM)
    anyspace = pl.BlockSpec(memory_space=pl.ANY)
    dma = pltpu.SemaphoreType.DMA
    small = jax.ShapeDtypeStruct((J, TR, TC), F32)
    return pl.pallas_call(
        kernel,
        out_shape=(small, small, jax.ShapeDtypeStruct((ITERS,), F32)),
        in_specs=[vmem, vmem, anyspace, vmem, smem, anyspace, smem, smem, vmem],
        out_specs=(vmem, vmem, smem),
        scratch_shapes=[
            pltpu.VMEM((2, NC, J, TR, TC, RC), BF16),
            pltpu.VMEM((ITERS, NC, 2, J, TC, RC), BF16),
            pltpu.VMEM((ITERS, NC, 2, J // 2, 2 * TR, RC), BF16),
            pltpu.VMEM((ITERS, NC, 2, J // 2, 2 * TR, RC), BF16),
            pltpu.VMEM((NC, J, M, RC), F32),
            pltpu.VMEM((J, M, RC), F32),
            pltpu.VMEM((J, M, 128), F32),
            pltpu.VMEM((M, RC), F32),
            pltpu.VMEM((M, RC), F32),
            pltpu.VMEM((2, 2, HM, 256), BF16),
            pltpu.VMEM((4, M, 128), F32),
            pltpu.VMEM((M, 128), F32),
            pltpu.VMEM((M, 128), F32),
            pltpu.VMEM((K, M, 128), F32),
            pltpu.VMEM((K, J, TR, TC), F32),
            pltpu.VMEM((M, 128), F32),
            pltpu.VMEM((M, 128), F32),
            pltpu.VMEM((M, 128), F32),
            pltpu.VMEM((ITERS, M, 128), F32),
            pltpu.VMEM((ITERS, 2, TR, 128), F32),
            pltpu.VMEM((ITERS, 2, TC, 128), F32),
            pltpu.VMEM((ITERS, 2, TR, 128), F32),
            pltpu.VMEM((2, TC, 128), F32),
            pltpu.VMEM((2, TR, 128), F32),
            pltpu.VMEM((M, 128), F32),
            pltpu.VMEM((ITERS, 2, 1, 128), F32),
            pltpu.VMEM((ITERS, NX, 1, 128), F32),
            pltpu.VMEM((ITERS, NY, 1, 128), F32),
            dma((NC,)),
            dma,
            dma((ITERS, NC, 4)),
            dma((ITERS, NC, 4)),
            dma((ITERS, 4)),
            dma((ITERS, 4)),
            dma((ITERS, NX)),
            dma((ITERS, NX)),
            dma((ITERS, NY)),
            dma((ITERS, NY)),
        ],
        compiler_params=pltpu.CompilerParams(
            collective_id=0, has_side_effects=True, vmem_limit_bytes=62 * 1024 * 1024
        ),
    )(*args)


def solution(mesh):
    tile = P(None, "gy", "gx")
    placed = (
        tile, tile, P(None, None, "gy", "gx"), P(), P(), P(None, "gy", "gx", None), P(), P(), tile,
    )
    return jax.shard_map(
        local, mesh=mesh, in_specs=placed, out_specs=(tile, tile, P()), check_vma=False
    )
```

profile of v0, /device:TPU:1, one launch (start us, length us, event | category | flops | bytes accessed | tf_op | source)
XLA Modules:
  0.0 193.5 jit_solution(12408568182395885728)
XLA Ops:
  0.6 188.6 %shard_map.112 = (f32[32,8,32]{2,1,0:T(8,128)}, f32[32,8,32]{2,1,0:T(8,128)}, f32[3]{0:T(128)}) custom-call(f32[32,8,32]{2,1,0:T(8,128)} %mean_in.1, f32[32,8,32]{2,1,0:T(8,128)} %obs_in.1, f32[4,32,8,32]{3,2,1,0:T(8,128)} %chars_in.1, f32[4,512]{1,0:T(4,128)} %draws_ref.1, f32[4]{0:T(128)} %scale_ref.1, bf16[32,8,32,512]{3,2,1,0:T(8,128)(2,1)} %prior_in.1, ...), custom_call_target="tpu_custom_call" | custom-call | tf_op jit(solution)/shard_map/pallas_call | solution.py:400
  189.2 1.6 copy.15
  190.8 1.6 copy.16
  192.3 1.1 copy.17
where the time goes:
time: 194 us; the launch traced here: 193 us
  Pallas kernels  189 us (97%)
  local copies, waits for them, and re-layouts  4.26 us (2%)
    pallas_call x1, Pallas kernels, local(): pl.pallas_call(kernel, out_shape=(small, small, jax.ShapeDtypeStruct((ITE...  189 us
    unnamed x3, local copies, waits for them, and re-layouts  4.26 us

commit v1 on v0

--- a/solution.py
+++ b/solution.py
@@ -16,10 +16,14 @@
 M = TR * TC
 HM = M // 2
 R = 512
-RC = 128
+RC = 256
 NC = R // RC
+NP = RC // 128
 NY = 16
 NX = 8
+BM = 64
+CUTS = (0, 24, 32)
+ALL = tuple(range(len(CUTS) - 1))
 LOG2E = math.log2(math.e)
 step_level = 0.2
 gap_eps = 1e-06
@@ -45,8 +49,8 @@
 def kernel(
     mean_in, obs_in, chars_in, draws_ref, scale_ref, prior_in, spill_ref, rate_ref, adj_ref,
     mean_out, log_out, gap_out,
-    st, hr, hc, cs, taste, ex, bx, den, rden, amat, aw, inv, gain, cz, char_buf,
-    zmean, zobs, zlog, zsend, zc_send, hz_r, hz_c, mh_r, mh_c, share, mxs, mxg, mxy,
+    st, hr, hc, cs, ex, den, rden, amat, near, far, lhs, chars_wide, draw_rows, aw, links, inv, gain,
+    char_buf, zmean, zobs, zsend, zc_send, hz_r, hz_c, mh_r, mh_c, share, mxs, mxg, mxy,
     prior_sem, char_sem, s_sem, r_sem, sz_sem, rz_sem, sg_sem, rg_sem, sy_sem, ry_sem,
 ):
     gy = lax.axis_index("gy")
@@ -78,21 +82,26 @@
     west = {"gx": lax.rem(gx + NX - 1, NX)}
     east = {"gx": lax.rem(gx + 1, NX)}
 
-    def edge_copies(e, c):
+    def edge_copies(e, c, pieces):
         b = e % 2
-        plan = (
-            (st.at[b, c, :, TR - 1], hr.at[e, c, 0], south),
-            (st.at[b, c, :, 0], hr.at[e, c, 1], north),
-            (cs.at[e, c, 1], hc.at[e, c, 0], east),
-            (cs.at[e, c, 0], hc.at[e, c, 1], west),
-        )
-        return [
-            pltpu.make_async_remote_copy(
-                src_ref=src, dst_ref=dst, send_sem=s_sem.at[e, c, k], recv_sem=r_sem.at[e, c, k],
-                device_id=to, device_id_type=MESH,
-            )
-            for k, (src, dst, to) in enumerate(plan)
-        ]
+        copies = []
+        for p in pieces:
+            js = pl.ds(CUTS[p], CUTS[p + 1] - CUTS[p])
+            qs = pl.ds(CUTS[p] // 2, (CUTS[p + 1] - CUTS[p]) // 2)
+            plan = (
+                (st.at[b, c, js, TR - 1], hr.at[e, c, 0, js], south),
+                (st.at[b, c, js, 0], hr.at[e, c, 1, js], north),
+                (cs.at[e, c, 1, qs], hc.at[e, c, 0, qs], east),
+                (cs.at[e, c, 0, qs], hc.at[e, c, 1, qs], west),
+            )
+            for k, (src, dst, to) in enumerate(plan):
+                copies.append(
+                    pltpu.make_async_remote_copy(
+                        src_ref=src, dst_ref=dst, send_sem=s_sem.at[e, c, p, k],
+                        recv_sem=r_sem.at[e, c, p, k], device_id=to, device_id_type=MESH,
+                    )
+                )
+        return copies
 
     def small_copies(x):
         plan = (
@@ -128,13 +137,22 @@
                 j = 2 * q + jj
                 value = st[0, c, j].reshape(M, RC).astype(F32) * spill_ref[j]
                 st[0, c, j] = value.astype(BF16).reshape(TR, TC, RC)
-                ex[j] = value
-                west_cols.append(ex[j, pl.ds(0, TR, stride=TC), :])
-                east_cols.append(ex[j, pl.ds(TC - 1, TR, stride=TC), :])
+                for part in range(NP):
+                    ex[j, part] = value[:, part * 128 : (part + 1) * 128]
+                for cols, first in ((west_cols, 0), (east_cols, TC - 1)):
+                    cols.append(
+                        jnp.concatenate(
+                            [
+                                ex[j, part, pl.ds(first, TR, stride=TC), :]
+                                for part in range(NP)
+                            ],
+                            axis=1,
+                        )
+                    )
             cs[0, c, 0, q] = jnp.concatenate(west_cols, axis=0).astype(BF16)
             cs[0, c, 1, q] = jnp.concatenate(east_cols, axis=0).astype(BF16)
 
-        for copy in edge_copies(0, c):
+        for copy in edge_copies(0, c, ALL):
             copy.start()
 
     eye = (row_iota((TC, TC)) == lane_iota((TC, TC))).astype(F32)
@@ -155,17 +173,18 @@
             line = adj_ref[k, pl.ds(row, 1), :].astype(F32)
             column = jnp.sum(jnp.where(eye > 0, line, 0.0), axis=1, keepdims=True)
             aw[k, pl.ds(row * TC, TC), :] = jnp.broadcast_to(column, (TC, 128))
-    links = jnp.maximum(aw[0] + aw[1] + aw[2] + aw[3], 1.0)
-    inverse = 1.0 / links
+    count = jnp.maximum(aw[0] + aw[1] + aw[2] + aw[3], 1.0)
+    links[...] = count
+    inverse = 1.0 / count
     inv[...] = inverse
-    gain[...] = inverse * LOG2E
-
-    @pl.loop(0, 4)
-    def _(i):
-        par = i // 2
-        h = i % 2
+    gain[...] = jnp.concatenate([inverse * LOG2E] * (RC // 128), axis=1)
+
+    @pl.loop(0, 2)
+    def _(h):
         shape = (HM, 128)
         at = row_iota(shape)
+        lane = lane_iota(shape)
+        block = lane >> 5
         col = at & (TC - 1)
         row = (at >> 5) + h * (TR // 2)
         mrows = pl.ds(pl.multiple_of(h * HM, HM), HM)
@@ -173,42 +192,66 @@
         w1 = jnp.where((row == TR - 1) & (gy == NY - 1), 0.0, aw[1, mrows, :])
         w2 = jnp.where((col == 0) & (gx == 0), 0.0, aw[2, mrows, :])
         w3 = jnp.where((col == TC - 1) & (gx == NX - 1), 0.0, aw[3, mrows, :])
-        west_slot = jnp.where(col == 0, 192 + par * TR + row, at + TC - 1)
-        east_slot = jnp.where(col == TC - 1, 208 + par * TR + row, at + TC + 1)
-        for part in range(2):
-            slot = lane_iota(shape) + part * 128
+
+        def entries(slot, par):
+            west_slot = jnp.where(col == 0, 192 + par * TR + row, at + TC - 1)
+            east_slot = jnp.where(col == TC - 1, 208 + par * TR + row, at + TC + 1)
             entry = jnp.where(slot == at, w0, 0.0)
             entry = entry + jnp.where(slot == at + 2 * TC, w1, 0.0)
             entry = entry + jnp.where(slot == west_slot, w2, 0.0)
-            entry = entry + jnp.where(slot == east_slot, w3, 0.0)
-            amat[par, h, :, pl.ds(part * 128, 128)] = entry.astype(BF16)
+            return entry + jnp.where(slot == east_slot, w3, 0.0)
+
+        first = entries(lane, 0)
+        amat[h, :, pl.ds(0, 128)] = first
+        near[h] = first.astype(BF16)
+        amat[h, :, pl.ds(128, 128)] = entries(lane + 128, 0)
+        for i in range(4):
+            slot = jnp.where(block > i, lane + 96, lane + 128)
+            far[i, h] = jnp.where(block == i, 0.0, entries(slot, i % 2))
+
+    def split(value):
+        high = value.astype(BF16)
+        rest = value - high.astype(F32)
+        middle = rest.astype(BF16)
+        return high, middle, (rest - middle.astype(F32)).astype(BF16)
+
+    def select_sum(parts, masks):
+        total = None
+        for part, mask in zip(parts, masks):
+            term = lax.dot_general(
+                part, mask.astype(F32).astype(BF16), (((1,), (0,)), ((), ())), preferred_element_type=F32
+            )
+            total = term if total is None else total + term
+        return total
 
     char_copy.wait()
-
-    @pl.loop(0, K)
-    def _(k):
-        for row in range(TR):
-            cz[k, pl.ds(row * TC, TC), :] = to_markets(char_buf[k, :, row, :])
-
-    draw_rows = [
-        [draws_ref[pl.ds(k, 1), pl.ds(c * RC, RC)] * (scale_ref[k] * LOG2E) for c in range(NC)]
-        for k in range(K)
-    ]
-
-    @pl.loop(0, J)
-    def _(j):
-        @pl.loop(0, TR)
-        def _(row):
-            rows = pl.ds(pl.multiple_of(row * TC, TC), TC)
-            here = lane_iota((TC, 128)) == j
-            columns = [
-                jnp.sum(jnp.where(here, cz[k, rows, :], 0.0), axis=1, keepdims=True) for k in range(K)
-            ]
-            for c in range(NC):
-                total = columns[0] * draw_rows[0][c]
-                for k in range(1, K):
-                    total = total + columns[k] * draw_rows[k][c]
-                taste[c, j, rows, :] = total
+    for row in range(TR):
+        block = jnp.concatenate([char_buf[k, :, row, :] for k in range(K)], axis=0)
+        rows = pl.ds(row * TC, TC)
+        ex[0, 0, rows, :] = exact_dot(eye, block, ((1,), (1,))) * links[rows, :]
+    char_parts = split(ex[0, 0])
+    source = row_iota((128, 128))
+    place = lane_iota((128, 128))
+    within = place & 31
+
+    @pl.loop(0, J // 4)
+    def _(b):
+        kept = ((source >> 5) == (within & 3)) & ((source & 31) == 4 * b + (place >> 5))
+        term = within >> 2
+        chars_wide[b] = select_sum(
+            char_parts,
+            (
+                kept & ((term == 0) | (term == 1) | (term == 4)),
+                kept & ((term == 2) | (term == 3)),
+                kept & (term == 5),
+            ),
+        )
+
+    scaled = jnp.concatenate([draws_ref[pl.ds(k, 1), :] * scale_ref[k] for k in range(K)], axis=0)
+    high, middle, low = (part.astype(F32) for part in split(scaled))
+    draw_rows[...] = jnp.concatenate(
+        [high, middle, high, middle, low, high, jnp.ones((3, R), F32), jnp.zeros((5, R), F32)], axis=0
+    ).astype(BF16)
 
     rates = jnp.zeros((1, 128), F32)
     for j in range(J):
@@ -217,7 +260,7 @@
     zero_rows = jnp.zeros((TR, 128), F32)
     zero_tail = jnp.zeros((32, 128), F32)
 
-    def largest(t, value):
+    def largest(t, value, meanwhile, afterwards):
         mxs[t, 0] = value
         mxg[t, gx] = value
 
@@ -249,6 +292,7 @@
 
         for d in range(1, NX):
             along_x(d).start()
+        meanwhile()
         for d in range(1, NX):
             from_x(d).wait_recv()
         best = mxg[t, 0]
@@ -258,6 +302,7 @@
         mxy[t, gy] = best
         for d in range(1, NY):
             along_y(d).start()
+        afterwards()
         for d in range(1, NY):
             from_y(d).wait_recv()
         best = mxy[t, 0]
@@ -278,6 +323,7 @@
         b = t % 2
         last = t == ITERS - 1
 
+        base = []
         mean_now = zmean[...]
         west_halo = [mh_c[0], zero_rows]
         east_halo = [mh_c[1], zero_rows]
@@ -287,88 +333,127 @@
             else:
                 pieces = [mean_now[3 * TC :], mh_r[1]]
             around = jnp.concatenate(pieces + west_halo + east_halo + [zero_tail], axis=0)
-            part = exact_dot(amat[0, h].astype(F32), around, ((1,), (0,)))
+            part = exact_dot(amat[h], around, ((1,), (0,)))
             rows = pl.ds(h * HM, HM)
-            zlog[rows, :] = (zmean[rows, :] + rates * (part * inv[rows, :])) * LOG2E
-
-        @pl.loop(0, J)
-        def _(j):
-            picked = jnp.where(lane_iota((M, 128)) == j, zlog[...], 0.0)
-            bx[j] = jnp.broadcast_to(jnp.sum(picked, axis=1, keepdims=True), (M, 128))
+            base.append((zmean[rows, :] + rates * (part * inv[rows, :])) * links[rows, :])
+        base_parts = split(jnp.concatenate(base, axis=0))
+
+        @pl.loop(0, J // 4)
+        def _(b):
+            kept = source == 4 * b + (place >> 5)
+            wide = chars_wide[b] + select_sum(
+                base_parts, tuple(kept & (within == 24 + x) for x in range(3))
+            )
+            here = lane_iota((HM, 128)) >> 5
+            for h in range(2):
+                for i in range(4):
+                    lhs[4 * b + i, h] = jnp.where(
+                        here == i, wide[h * HM : (h + 1) * HM], far[i, h]
+                    ).astype(BF16)
 
         share[...] = jnp.zeros((M, 128), F32)
 
         @pl.loop(0, NC)
         def _(c):
-            for copy in edge_copies(t, c):
+            for copy in edge_copies(t, c, ALL):
                 copy.wait_recv()
             den[...] = jnp.ones((M, RC), F32)
 
-            @pl.loop(0, J // 2)
-            def _(q):
-                halo_cols = [hc[t, c, 0, q], hc[t, c, 1, q], jnp.zeros((32, RC), BF16)]
+            draws_now = draw_rows[:, pl.ds(pl.multiple_of(c * RC, RC), RC)]
+
+            @pl.loop(0, J // 4)
+            def _(b4):
                 for h in range(2):
                     rows = pl.ds(h * HM, HM)
-                    total = den[rows, :]
-                    for jj in range(2):
-                        j = 2 * q + jj
-                        if h == 0:
-                            pieces = [hr[t, c, 0, j], st[b, c, j, pl.ds(0, 5)].reshape(5 * TC, RC)]
-                        else:
-                            pieces = [st[b, c, j, pl.ds(3, 5)].reshape(5 * TC, RC), hr[t, c, 1, j]]
-                        around = jnp.concatenate(pieces + halo_cols, axis=0)
-                        spill = lax.dot_general(
-                            amat[jj, h], around, (((1,), (0,)), ((), ())), preferred_element_type=F32
-                        )
-                        power = spill * gain[rows, :] + (taste[c, j, rows, :] + bx[j, rows, :])
-                        value = jnp.exp2(power)
-                        ex[j, rows, :] = value
-                        total = total + value
-                    den[rows, :] = total
-
-            rden[...] = 1.0 / den[...]
+                    for pair in range(2):
+                        q = 2 * b4 + pair
+                        sides = jnp.concatenate([hc[t, c, 0, q], hc[t, c, 1, q]], axis=0)
+                        total = den[rows, :]
+                        for i in (2 * pair, 2 * pair + 1):
+                            j = 4 * b4 + i
+                            if h == 0:
+                                pieces = [hr[t, c, 0, j]] + [st[b, c, j, r] for r in range(5)]
+                            else:
+                                pieces = [st[b, c, j, r] for r in range(3, 8)] + [hr[t, c, 1, j]]
+                            pieces = pieces + [sides]
+                            pieces = pieces[: 4 + i] + [draws_now] + pieces[4 + i :]
+                            left = jnp.concatenate([near[h], lhs[j, h]], axis=1)
+                            summed = lax.dot_general(
+                                left, jnp.concatenate(pieces, axis=0), (((1,), (0,)), ((), ())),
+                                preferred_element_type=F32,
+                            )
+                            value = jnp.exp2(summed * gain[rows, :])
+                            for part in range(NP):
+                                ex[j, part, rows, :] = value[:, part * 128 : (part + 1) * 128]
+                            total = total + value
+                        den[rows, :] = total
+
+            for part in range(NP):
+                rden[part] = 1.0 / den[:, part * 128 : (part + 1) * 128]
             if t == 1:
-                for copy in edge_copies(0, c):
+                for copy in edge_copies(0, c, ALL):
                     copy.wait_send()
 
-            @pl.loop(0, J // 2)
-            def _(q):
-                west_cols = []
-                east_cols = []
-                for jj in range(2):
-                    j = 2 * q + jj
-                    for h in range(2):
-                        rows = pl.ds(h * HM, HM)
-                        prob = ex[j, rows, :] * rden[rows, :]
-                        here = lane_iota((HM, 128)) == j
-                        share[rows, :] += jnp.where(here, jnp.sum(prob, axis=1, keepdims=True), 0.0)
+            @pl.loop(0, J // 4)
+            def _(b4):
+                lane = lane_iota((BM, 128))
+                for m0 in range(0, M, BM):
+                    rows = pl.ds(m0, BM)
+                    found = share[rows, :]
+                    for i in range(4):
+                        j = 4 * b4 + i
+                        probs = [ex[j, part, rows, :] * rden[part, rows, :] for part in range(NP)]
+                        folded = probs[0]
+                        for prob in probs[1:]:
+                            folded = folded + prob
+                        found = found + jnp.where(lane == j, jnp.sum(folded, axis=1, keepdims=True), 0.0)
                         if not last:
-                            st[1 - b, c, j, pl.ds(h * (TR // 2), TR // 2)] = (
-                                (prob * spill_ref[j]).astype(BF16).reshape(TR // 2, TC, RC)
-                            )
-                    if not last:
-                        for cols, first in ((west_cols, 0), (east_cols, TC - 1)):
+                            for part, prob in enumerate(probs):
+                                lanes = pl.ds(part * 128, 128)
+                                st[1 - b, c, j, pl.ds(m0 // TC, BM // TC), :, lanes] = (
+                                    (prob * spill_ref[j]).astype(BF16).reshape(BM // TC, TC, 128)
+                                )
+                    share[rows, :] = found
+                if not last:
+                    for pair in range(2):
+                        for side, first in ((0, 0), (1, TC - 1)):
                             at = pl.ds(first, TR, stride=TC)
-                            cols.append(ex[j, at, :] * rden[at, :] * spill_ref[j])
-                if not last:
-                    cs[t + 1, c, 0, q] = jnp.concatenate(west_cols, axis=0).astype(BF16)
-                    cs[t + 1, c, 1, q] = jnp.concatenate(east_cols, axis=0).astype(BF16)
+                            cols = []
+                            for j in (4 * b4 + 2 * pair, 4 * b4 + 2 * pair + 1):
+                                for part in range(NP):
+                                    cols.append(ex[j, part, at, :] * rden[part, at, :] * spill_ref[j])
+                            cs[t + 1, c, side, 2 * b4 + pair] = jnp.concatenate(
+                                [jnp.concatenate(cols[:NP], axis=1), jnp.concatenate(cols[NP:], axis=1)], axis=0
+                            ).astype(BF16)
 
             if not last:
-                for copy in edge_copies(t + 1, c):
-                    copy.start()
+                @pl.when(c == 0)
+                def _():
+                    for copy in edge_copies(t + 1, 0, ALL[:1]):
+                        copy.start()
 
         log_share = jnp.log(jnp.where(real, share[...] * (1.0 / R), 1.0))
         residual = jnp.where(real, zobs[...] - log_share, 0.0)
         if not last:
             send_small(t + 1, residual)
         gap = jnp.max(jnp.max(jnp.abs(residual), axis=0, keepdims=True), axis=1, keepdims=True)
-        if last:
-            for row in range(TR):
-                log_out[:, row, :] = exact_dot(
-                    eye_wide, log_share[row * TC : (row + 1) * TC], ((1,), (1,))
-                )
-        best = largest(t, jnp.broadcast_to(gap, (1, 128)))
+
+        def meanwhile():
+            if last:
+                for row in range(TR):
+                    log_out[:, row, :] = exact_dot(
+                        eye_wide, log_share[row * TC : (row + 1) * TC], ((1,), (1,))
+                    )
+
+        def afterwards():
+            if not last:
+                for copy in edge_copies(t + 1, 0, ALL[1:]):
+                    copy.start()
+                for c in range(1, NC):
+                    for copy in edge_copies(t + 1, c, ALL):
+                        copy.start()
+
+        best = largest(t, jnp.broadcast_to(gap, (1, 128)), meanwhile, afterwards)
         gap_out[t] = jnp.max(best)
         step = step_level / (best + gap_eps)
         mean_now = zmean[...] + step * residual
@@ -387,7 +472,7 @@
     for e in range(1, ITERS):
         @pl.loop(0, NC)
         def _(c):
-            for copy in edge_copies(e, c):
+            for copy in edge_copies(e, c, ALL):
                 copy.wait_send()
 
 
@@ -407,18 +492,20 @@
             pltpu.VMEM((ITERS, NC, 2, J, TC, RC), BF16),
             pltpu.VMEM((ITERS, NC, 2, J // 2, 2 * TR, RC), BF16),
             pltpu.VMEM((ITERS, NC, 2, J // 2, 2 * TR, RC), BF16),
-            pltpu.VMEM((NC, J, M, RC), F32),
-            pltpu.VMEM((J, M, RC), F32),
-            pltpu.VMEM((J, M, 128), F32),
+            pltpu.VMEM((J, NP, M, 128), F32),
             pltpu.VMEM((M, RC), F32),
-            pltpu.VMEM((M, RC), F32),
-            pltpu.VMEM((2, 2, HM, 256), BF16),
+            pltpu.VMEM((NP, M, 128), F32),
+            pltpu.VMEM((2, HM, 256), F32),
+            pltpu.VMEM((2, HM, 128), BF16),
+            pltpu.VMEM((4, 2, HM, 128), F32),
+            pltpu.VMEM((J, 2, HM, 128), BF16),
+            pltpu.VMEM((J // 4, M, 128), F32),
+            pltpu.VMEM((32, R), BF16),
             pltpu.VMEM((4, M, 128), F32),
             pltpu.VMEM((M, 128), F32),
             pltpu.VMEM((M, 128), F32),
-            pltpu.VMEM((K, M, 128), F32),
+            pltpu.VMEM((M, RC), F32),
             pltpu.VMEM((K, J, TR, TC), F32),
-            pltpu.VMEM((M, 128), F32),
             pltpu.VMEM((M, 128), F32),
             pltpu.VMEM((M, 128), F32),
             pltpu.VMEM((ITERS, M, 128), F32),
@@ -433,8 +520,8 @@
             pltpu.VMEM((ITERS, NY, 1, 128), F32),
             dma((NC,)),
             dma,
-            dma((ITERS, NC, 4)),
-            dma((ITERS, NC, 4)),
+            dma((ITERS, NC, len(CUTS) - 1, 4)),
+            dma((ITERS, NC, len(CUTS) - 1, 4)),
             dma((ITERS, 4)),
             dma((ITERS, 4)),
             dma((ITERS, NX)),

time: 194 us -> 152 us (0.78)
  Pallas kernels: 189 us -> 147 us
    pallas_call x1, Pallas kernels: 189 us -> 147 us  [local(): pl.pallas_call(kernel, out_shape=(small, small, jax.ShapeDtypeStruct((ITE...]
where the time goes in v1:
time: 152 us; the launch traced here: 151 us
  Pallas kernels  147 us (97%)
  local copies, waits for them, and re-layouts  4.26 us (3%)
    pallas_call x1, Pallas kernels, local(): pl.pallas_call(kernel, out_shape=(small, small, jax.ShapeDtypeStruct((ITE...  147 us
    unnamed x3, local copies, waits for them, and re-layouts  4.26 us

profile of v1, /device:TPU:1, one launch (start us, length us, event | category | flops | bytes accessed | tf_op | source)
XLA Modules:
  0.0 151.4 jit_solution(6899136703417275490)
XLA Ops:
  0.6 146.5 %shard_map.112 = (f32[32,8,32]{2,1,0:T(8,128)}, f32[32,8,32]{2,1,0:T(8,128)}, f32[3]{0:T(128)}) custom-call(f32[32,8,32]{2,1,0:T(8,128)} %mean_in.1, f32[32,8,32]{2,1,0:T(8,128)} %obs_in.1, f32[4,32,8,32]{3,2,1,0:T(8,128)} %chars_in.1, f32[4,512]{1,0:T(4,128)} %draws_ref.1, f32[4]{0:T(128)} %scale_ref.1, bf16[32,8,32,512]{3,2,1,0:T(8,128)(2,1)} %prior_in.1, ...), custom_call_target="tpu_custom_call" | custom-call | tf_op jit(solution)/shard_map/pallas_call | solution.py:485
  147.2 1.6 %copy.15 = f32[32,8,32]{2,1,0:T(8,128)} copy(f32[32,8,32]{2,1,0:T(8,128)} %get-tuple-element.6) | data formatting | bytes 65536
  148.7 1.6 %copy.16 = f32[32,8,32]{2,1,0:T(8,128)} copy(f32[32,8,32]{2,1,0:T(8,128)} %get-tuple-element.7) | data formatting | bytes 65536
  150.3 1.1 copy.17

commit v2 on v1

--- a/solution.py
+++ b/solution.py
@@ -22,7 +22,7 @@
 NY = 16
 NX = 8
 BM = 64
-CUTS = (0, 24, 32)
+CUTS = (0, 16, 20, 32)
 ALL = tuple(range(len(CUTS) - 1))
 LOG2E = math.log2(math.e)
 step_level = 0.2
@@ -61,10 +61,8 @@
             prior_in.at[:, :, :, pl.ds(pl.multiple_of(c * RC, RC), RC)], st.at[0, c], prior_sem.at[c]
         )
 
-    for c in range(NC):
-        prior_copy(c).start()
+    prior_copy(0).start()
     char_copy = pltpu.make_async_copy(chars_in, char_buf, char_sem)
-    char_copy.start()
 
     barrier = pltpu.get_barrier_semaphore()
     for d in range(1, NX):
@@ -82,19 +80,26 @@
     west = {"gx": lax.rem(gx + NX - 1, NX)}
     east = {"gx": lax.rem(gx + 1, NX)}
 
-    def edge_copies(e, c, pieces):
+    def edge_copies(e, c, pieces, sides=(0, 1, 2, 3)):
         b = e % 2
         copies = []
-        for p in pieces:
-            js = pl.ds(CUTS[p], CUTS[p + 1] - CUTS[p])
-            qs = pl.ds(CUTS[p] // 2, (CUTS[p + 1] - CUTS[p]) // 2)
+        cuts = CUTS if e else (0, J)
+        for p in pieces if e else (0,):
+            js = pl.ds(cuts[p], cuts[p + 1] - cuts[p])
+            qs = pl.ds(cuts[p] // 2, (cuts[p + 1] - cuts[p]) // 2)
+            if e:
+                last_row, first_row = st.at[b, c, js, TR - 1], st.at[b, c, js, 0]
+            else:
+                lanes = pl.ds(pl.multiple_of(c * RC, RC), RC)
+                last_row, first_row = prior_in.at[:, TR - 1, :, lanes], prior_in.at[:, 0, :, lanes]
             plan = (
-                (st.at[b, c, js, TR - 1], hr.at[e, c, 0, js], south),
-                (st.at[b, c, js, 0], hr.at[e, c, 1, js], north),
+                (last_row, hr.at[e, c, 0, js], south),
+                (first_row, hr.at[e, c, 1, js], north),
                 (cs.at[e, c, 1, qs], hc.at[e, c, 0, qs], east),
                 (cs.at[e, c, 0, qs], hc.at[e, c, 1, qs], west),
             )
-            for k, (src, dst, to) in enumerate(plan):
+            for k in sides:
+                src, dst, to = plan[k]
                 copies.append(
                     pltpu.make_async_remote_copy(
                         src_ref=src, dst_ref=dst, send_sem=s_sem.at[e, c, p, k],
@@ -124,6 +129,12 @@
         zc_send[x, 1] = zsend[x, pl.ds(TC - 1, TR, stride=TC), :]
         for copy in small_copies(x):
             copy.start()
+
+    for copy in edge_copies(0, 0, ALL, (0, 1)):
+        copy.start()
+    for c in range(1, NC):
+        prior_copy(c).start()
+    char_copy.start()
 
     @pl.loop(0, NC)
     def _(c):
@@ -152,8 +163,13 @@
             cs[0, c, 0, q] = jnp.concatenate(west_cols, axis=0).astype(BF16)
             cs[0, c, 1, q] = jnp.concatenate(east_cols, axis=0).astype(BF16)
 
-        for copy in edge_copies(0, c, ALL):
+        for copy in edge_copies(0, c, ALL, (2, 3)):
             copy.start()
+
+        @pl.when(c + 1 < NC)
+        def _():
+            for copy in edge_copies(0, c + 1, ALL, (0, 1)):
+                copy.start()
 
     eye = (row_iota((TC, TC)) == lane_iota((TC, TC))).astype(F32)
     eye_wide = (row_iota((J, 128)) == lane_iota((J, 128))).astype(F32)
@@ -371,10 +387,13 @@
                         total = den[rows, :]
                         for i in (2 * pair, 2 * pair + 1):
                             j = 4 * b4 + i
+                            halo = hr[t, c, h, j]
+                            if t == 0:
+                                halo = (halo.astype(F32) * spill_ref[j]).astype(BF16)
                             if h == 0:
-                                pieces = [hr[t, c, 0, j]] + [st[b, c, j, r] for r in range(5)]
+                                pieces = [halo] + [st[b, c, j, r] for r in range(5)]
                             else:
-                                pieces = [st[b, c, j, r] for r in range(3, 8)] + [hr[t, c, 1, j]]
+                                pieces = [st[b, c, j, r] for r in range(3, 8)] + [halo]
                             pieces = pieces + [sides]
                             pieces = pieces[: 4 + i] + [draws_now] + pieces[4 + i :]
                             left = jnp.concatenate([near[h], lhs[j, h]], axis=1)
@@ -439,6 +458,9 @@
         gap = jnp.max(jnp.max(jnp.abs(residual), axis=0, keepdims=True), axis=1, keepdims=True)
 
         def meanwhile():
+            if not last:
+                for copy in edge_copies(t + 1, 0, ALL[1:2]):
+                    copy.start()
             if last:
                 for row in range(TR):
                     log_out[:, row, :] = exact_dot(
@@ -447,7 +469,7 @@
 
         def afterwards():
             if not last:
-                for copy in edge_copies(t + 1, 0, ALL[1:]):
+                for copy in edge_copies(t + 1, 0, ALL[2:]):
                     copy.start()
                 for c in range(1, NC):
                     for copy in edge_copies(t + 1, c, ALL):
@@ -476,15 +498,23 @@
                 copy.wait_send()
 
 
+def put_out(mean_ref, log_ref, gap_ref, mean_out, log_out, gap_out):
+    mean_out[...] = mean_ref[...]
+    log_out[...] = log_ref[...]
+    for t in range(ITERS):
+        gap_out[t] = gap_ref[t]
+
+
 def local(*args):
     vmem = pl.BlockSpec(memory_space=pltpu.VMEM)
     smem = pl.BlockSpec(memory_space=pltpu.SMEM)
     anyspace = pl.BlockSpec(memory_space=pl.ANY)
     dma = pltpu.SemaphoreType.DMA
     small = jax.ShapeDtypeStruct((J, TR, TC), F32)
-    return pl.pallas_call(
+    out_shape = (small, small, jax.ShapeDtypeStruct((ITERS,), F32))
+    found = pl.pallas_call(
         kernel,
-        out_shape=(small, small, jax.ShapeDtypeStruct((ITERS,), F32)),
+        out_shape=out_shape,
         in_specs=[vmem, vmem, anyspace, vmem, smem, anyspace, smem, smem, vmem],
         out_specs=(vmem, vmem, smem),
         scratch_shapes=[
@@ -533,6 +563,9 @@
             collective_id=0, has_side_effects=True, vmem_limit_bytes=62 * 1024 * 1024
         ),
     )(*args)
+    return pl.pallas_call(
+        put_out, out_shape=out_shape, in_specs=[vmem, vmem, smem], out_specs=(vmem, vmem, smem)
+    )(*found)
 
 
 def solution(mesh):

time: 152 us -> 145 us (0.954)
  local copies, waits for them, and re-layouts: 4.26 us -> 0 us
  Pallas kernels: 147 us -> 145 us
    unnamed x3 -> x0, local copies, waits for them, and re-layouts: 4.26 us -> none
    pallas_call x1 -> x2, Pallas kernels: 147 us -> 145 us  [the longest x1 143 us: local(): pl.pallas_call(kernel, out_shape=out_shape, in_specs=[vmem, vmem, anyspac...]
where the time goes in v2:
time: 145 us
  Pallas kernels  145 us (100%)
    pallas_call x1, Pallas kernels, local(): pl.pallas_call(kernel, out_shape=out_shape, in_specs=[vmem, vmem, anyspac...  143 us

profile of v2, /device:TPU:1, one launch (start us, length us, event | category | flops | bytes accessed | tf_op | source)
XLA Modules:
  0.0 145.2 jit_solution(9487668591916811621)
XLA Ops:
  0.6 142.9 %shard_map.112 = (f32[32,8,32]{2,1,0:T(8,128)}, f32[32,8,32]{2,1,0:T(8,128)}, f32[3]{0:T(128)}) custom-call(f32[32,8,32]{2,1,0:T(8,128)} %mean_in.1, f32[32,8,32]{2,1,0:T(8,128)} %obs_in.1, f32[4,32,8,32]{3,2,1,0:T(8,128)} %chars_in.1, f32[4,512]{1,0:T(4,128)} %draws_ref.1, f32[4]{0:T(128)} %scale_ref.1, bf16[32,8,32,512]{3,2,1,0:T(8,128)(2,1)} %prior_in.1, ...), custom_call_target="tpu_custom_call" | custom-call | tf_op jit(solution)/shard_map/pallas_call | solution.py:515
  143.6 1.7 %shard_map.113 = (f32[32,8,32]{2,1,0:T(8,128)}, f32[32,8,32]{2,1,0:T(8,128)}, f32[3]{0:T(128)}) custom-call(f32[32,8,32]{2,1,0:T(8,128)} %get-tuple-element.6.mean_ref, f32[32,8,32]{2,1,0:T(8,128)} %get-tuple-element.7.log_ref, f32[3]{0:T(128)} %get-tuple-element.8.gap_ref), custom_call_target="tpu_custom_call" | custom-call | tf_op jit(solution)/shard_map/pallas_call | solution.py:566

commit v3 on v2

--- a/solution.py
+++ b/solution.py
@@ -22,7 +22,7 @@
 NY = 16
 NX = 8
 BM = 64
-CUTS = (0, 16, 20, 32)
+CUTS = (0, 16, 28, 32)
 ALL = tuple(range(len(CUTS) - 1))
 LOG2E = math.log2(math.e)
 step_level = 0.2
@@ -83,15 +83,14 @@
     def edge_copies(e, c, pieces, sides=(0, 1, 2, 3)):
         b = e % 2
         copies = []
-        cuts = CUTS if e else (0, J)
-        for p in pieces if e else (0,):
-            js = pl.ds(cuts[p], cuts[p + 1] - cuts[p])
-            qs = pl.ds(cuts[p] // 2, (cuts[p + 1] - cuts[p]) // 2)
+        for p in pieces:
+            js = pl.ds(CUTS[p], CUTS[p + 1] - CUTS[p])
+            qs = pl.ds(CUTS[p] // 2, (CUTS[p + 1] - CUTS[p]) // 2)
             if e:
                 last_row, first_row = st.at[b, c, js, TR - 1], st.at[b, c, js, 0]
             else:
                 lanes = pl.ds(pl.multiple_of(c * RC, RC), RC)
-                last_row, first_row = prior_in.at[:, TR - 1, :, lanes], prior_in.at[:, 0, :, lanes]
+                last_row, first_row = prior_in.at[js, TR - 1, :, lanes], prior_in.at[js, 0, :, lanes]
             plan = (
                 (last_row, hr.at[e, c, 0, js], south),
                 (first_row, hr.at[e, c, 1, js], north),
@@ -371,14 +370,18 @@
 
         @pl.loop(0, NC)
         def _(c):
-            for copy in edge_copies(t, c, ALL):
-                copy.wait_recv()
             den[...] = jnp.ones((M, RC), F32)
 
             draws_now = draw_rows[:, pl.ds(pl.multiple_of(c * RC, RC), RC)]
 
             @pl.loop(0, J // 4)
             def _(b4):
+                for p in ALL:
+                    @pl.when(b4 == CUTS[p] // 4)
+                    def _(p=p):
+                        for copy in edge_copies(t, c, (p,)):
+                            copy.wait_recv()
+
                 for h in range(2):
                     rows = pl.ds(h * HM, HM)
                     for pair in range(2):

time: 145 us -> 141 us (0.972)
  Pallas kernels: 145 us -> 141 us
    pallas_call x1, Pallas kernels: 143 us -> 139 us  [local(): pl.pallas_call(kernel, out_shape=out_shape, in_specs=[vmem, vmem, anyspac...]
where the time goes in v3:
time: 141 us
  Pallas kernels  141 us (100%)
    pallas_call x1, Pallas kernels, local(): pl.pallas_call(kernel, out_shape=out_shape, in_specs=[vmem, vmem, anyspac...  139 us

profile of v3, /device:TPU:1, one launch (start us, length us, event | category | flops | bytes accessed | tf_op | source)
XLA Modules:
  0.0 141.2 jit_solution(3455928701183929460)
XLA Ops:
  0.6 138.9 %shard_map.112 = (f32[32,8,32]{2,1,0:T(8,128)}, f32[32,8,32]{2,1,0:T(8,128)}, f32[3]{0:T(128)}) custom-call(f32[32,8,32]{2,1,0:T(8,128)} %mean_in.1, f32[32,8,32]{2,1,0:T(8,128)} %obs_in.1, f32[4,32,8,32]{3,2,1,0:T(8,128)} %chars_in.1, f32[4,512]{1,0:T(4,128)} %draws_ref.1, f32[4]{0:T(128)} %scale_ref.1, bf16[32,8,32,512]{3,2,1,0:T(8,128)(2,1)} %prior_in.1, ...), custom_call_target="tpu_custom_call" | custom-call | tf_op jit(solution)/shard_map/pallas_call | solution.py:518
  139.5 1.7 %shard_map.113 = (f32[32,8,32]{2,1,0:T(8,128)}, f32[32,8,32]{2,1,0:T(8,128)}, f32[3]{0:T(128)}) custom-call(f32[32,8,32]{2,1,0:T(8,128)} %get-tuple-element.6.mean_ref, f32[32,8,32]{2,1,0:T(8,128)} %get-tuple-element.7.log_ref, f32[3]{0:T(128)} %get-tuple-element.8.gap_ref), custom_call_target="tpu_custom_call" | custom-call | tf_op jit(solution)/shard_map/pallas_call | solution.py:569

commit v4 on v3

--- a/solution.py
+++ b/solution.py
@@ -47,10 +47,10 @@
 
 
 def kernel(
-    mean_in, obs_in, chars_in, draws_ref, scale_ref, prior_in, spill_ref, rate_ref, adj_ref,
+    mean_hbm, obs_hbm, chars_in, draws_hbm, scale_ref, prior_in, spill_ref, rate_ref, adj_hbm,
     mean_out, log_out, gap_out,
     st, hr, hc, cs, ex, den, rden, amat, near, far, lhs, chars_wide, draw_rows, aw, links, inv, gain,
-    char_buf, zmean, zobs, zsend, zc_send, hz_r, hz_c, mh_r, mh_c, share, mxs, mxg, mxy,
+    char_buf, mean_in, obs_in, draws_ref, adj_ref, small_sem, zmean, zobs, zsend, zc_send, hz_r, hz_c, mh_r, mh_c, share, mxs, mxg, mxy,
     prior_sem, char_sem, s_sem, r_sem, sz_sem, rz_sem, sg_sem, rg_sem, sy_sem, ry_sem,
 ):
     gy = lax.axis_index("gy")
@@ -134,6 +134,14 @@
     for c in range(1, NC):
         prior_copy(c).start()
     char_copy.start()
+    inputs = [
+        pltpu.make_async_copy(src, dst, small_sem.at[k])
+        for k, (src, dst) in enumerate(
+            ((mean_hbm, mean_in), (obs_hbm, obs_in), (draws_hbm, draws_ref), (adj_hbm, adj_ref))
+        )
+    ]
+    for copy in inputs:
+        copy.start()
 
     @pl.loop(0, NC)
     def _(c):
@@ -170,6 +178,9 @@
             for copy in edge_copies(0, c + 1, ALL, (0, 1)):
                 copy.start()
 
+    for copy in inputs:
+        copy.wait()
+
     eye = (row_iota((TC, TC)) == lane_iota((TC, TC))).astype(F32)
     eye_wide = (row_iota((J, 128)) == lane_iota((J, 128))).astype(F32)
     pad = jnp.zeros((128 - J, TC), F32)
@@ -323,10 +334,6 @@
         best = mxy[t, 0]
         for k in range(1, NY):
             best = jnp.maximum(best, mxy[t, k])
-        for d in range(1, NX):
-            along_x(d).wait_send()
-        for d in range(1, NY):
-            along_y(d).wait_send()
         return best
 
     for copy in small_copies(0):
@@ -494,6 +501,17 @@
                     eye_wide, mean_now[row * TC : (row + 1) * TC], ((1,), (1,))
                 )
 
+    for t in range(ITERS):
+        for d in range(1, NX):
+            pltpu.make_async_remote_copy(
+                src_ref=mxs.at[t, 0], dst_ref=mxg.at[t, gx], send_sem=sg_sem.at[t, d],
+                recv_sem=rg_sem.at[t, gx], device_id={"gx": lax.rem(gx + d, NX)}, device_id_type=MESH,
+            ).wait_send()
+        for d in range(1, NY):
+            pltpu.make_async_remote_copy(
+                src_ref=mxs.at[t, 1], dst_ref=mxy.at[t, gy], send_sem=sy_sem.at[t, d],
+                recv_sem=ry_sem.at[t, gy], device_id={"gy": lax.rem(gy + d, NY)}, device_id_type=MESH,
+            ).wait_send()
     for e in range(1, ITERS):
         @pl.loop(0, NC)
         def _(c):
@@ -518,7 +536,7 @@
     found = pl.pallas_call(
         kernel,
         out_shape=out_shape,
-        in_specs=[vmem, vmem, anyspace, vmem, smem, anyspace, smem, smem, vmem],
+        in_specs=[anyspace] * 4 + [smem, anyspace, smem, smem, anyspace],
         out_specs=(vmem, vmem, smem),
         scratch_shapes=[
             pltpu.VMEM((2, NC, J, TR, TC, RC), BF16),
@@ -539,6 +557,11 @@
             pltpu.VMEM((M, 128), F32),
             pltpu.VMEM((M, RC), F32),
             pltpu.VMEM((K, J, TR, TC), F32),
+            pltpu.VMEM((J, TR, TC), F32),
+            pltpu.VMEM((J, TR, TC), F32),
+            pltpu.VMEM((K, R), F32),
+            pltpu.VMEM((4, TR, TC), jnp.int32),
+            dma((4,)),
             pltpu.VMEM((M, 128), F32),
             pltpu.VMEM((M, 128), F32),
             pltpu.VMEM((ITERS, M, 128), F32),

time: 141 us -> 141 us (level)
  no operation moved by 1% of the time
where the time goes in v4:
time: 141 us
  Pallas kernels  140 us (99%)
    pallas_call x1, Pallas kernels, local(): pl.pallas_call(kernel, out_shape=out_shape, in_specs=[anyspace] * 4 + [sm...  139 us

profile of v4, /device:TPU:1, one launch (start us, length us, event | category | flops | bytes accessed | tf_op | source)
XLA Modules:
  0.0 141.0 jit_solution(5418816161469487130)
XLA Ops:
  0.6 138.7 %shard_map.112 = (f32[32,8,32]{2,1,0:T(8,128)}, f32[32,8,32]{2,1,0:T(8,128)}, f32[3]{0:T(128)}) custom-call(f32[32,8,32]{2,1,0:T(8,128)} %mean_hbm.1, f32[32,8,32]{2,1,0:T(8,128)} %obs_hbm.1, f32[4,32,8,32]{3,2,1,0:T(8,128)} %chars_in.1, f32[4,512]{1,0:T(4,128)} %draws_hbm.1, f32[4]{0:T(128)} %scale_ref.1, bf16[32,8,32,512]{3,2,1,0:T(8,128)(2,1)} %prior_in.1, ...), custom_call_target="tpu_custom_call" | custom-call | tf_op jit(solution)/shard_map/pallas_call | solution.py:536
  139.3 1.7 %shard_map.113 = (f32[32,8,32]{2,1,0:T(8,128)}, f32[32,8,32]{2,1,0:T(8,128)}, f32[3]{0:T(128)}) custom-call(f32[32,8,32]{2,1,0:T(8,128)} %get-tuple-element.6.mean_ref, f32[32,8,32]{2,1,0:T(8,128)} %get-tuple-element.7.log_ref, f32[3]{0:T(128)} %get-tuple-element.8.gap_ref), custom_call_target="tpu_custom_call" | custom-call | tf_op jit(solution)/shard_map/pallas_call | solution.py:592
